TPU v7x, 1024 devices: a whole 4x4x32 slice. The times are simulated.
1024 devices in a mesh: region: 64 (over z, core), mp: 16 (over y, x).
Axes of the slice: x: 4, y: 4, z: 32, core: 2. Of those that a mesh axis runs over, the one named last changes fastest.
Arguments:
- observations: bfloat16 [64, 64, 64, 256], P('region'), may hold values from -8 to 8
- cotangent: bfloat16 [64, 64, 16, 2048], P('region', None, 'mp'), may hold values from -96 to 96
- keys_values: bfloat16 [2, 512, 32768], P(None, 'mp', 'region'), may hold values from -6 to 6
- query_weight: bfloat16 [512, 256], P('mp'), may hold values from -1 to 1
- counts: int32 [64, 64], replicated, may hold values from 0 to 64, as said below
Outputs:
- pair_grad: float32 [2, 512, 32768], P(None, 'mp', 'region')
- projection_grad: float32 [512, 256], P('mp')
Inputs may be any that keep to these rules, and one draw needn't show every extreme that they name: counts[s, d] live observations lead block [s, d]; later slots are padding. Every region has a full block from some ingest shard, and some region has full blocks from every ingest shard.
All inputs are finite; a program needn't handle non-finite values.
Results may differ from a plain program's by a relative error of at most 0.008.
The roundings to bfloat16 on the way count: a program that leaves them out, or rounds other values in their place, can miss the bound.
Values may be sent and summed in bfloat16 or wider, within the bound.
A program may use at most 32 MiB of HBM per device.

v0:
```python
import math

import jax
import jax.numpy as jnp
from jax import lax
from jax.sharding import PartitionSpec as P

HEAD_DIM = 32


def passed_along(array, axis, by):
    peers = lax.axis_size(axis)
    return lax.ppermute(array, axis, [(i, (i + by) % peers) for i in range(peers)])


def per_device(observations, cotangent, keys_values, query_weight, counts):
    regions = lax.axis_size("region")
    region_id = lax.axis_index("region")
    capacity = observations.shape[2]
    width = observations.shape[3]
    local_heads = query_weight.shape[0] // HEAD_DIM
    all_rows = regions * capacity
    latent = keys_values.shape[2]
    scale_back = 1.0 / math.sqrt(HEAD_DIM)
    weight_heads = query_weight.reshape(local_heads, HEAD_DIM, width)
    arrived, arrived_grad = (
        lax.all_to_all(observations, "region", split_axis=1, concat_axis=0, tiled=True),
        lax.all_to_all(cotangent, "region", split_axis=1, concat_axis=0, tiled=True),
    )
    feature_rows = arrived.reshape(all_rows, width)
    queries = jnp.einsum(
        "rf,hef->hre", feature_rows, weight_heads, preferred_element_type=jnp.float32
    ).astype(jnp.bfloat16)
    counts_here = lax.dynamic_index_in_dim(counts, region_id, 1, keepdims=False)
    present = jnp.arange(capacity, dtype=jnp.int32)[None, :] < counts_here[:, None]
    out_grad = arrived_grad.reshape(regions, local_heads, capacity, HEAD_DIM)
    out_grad = jnp.where(present[:, None, :, None], out_grad, jnp.zeros((), jnp.bfloat16))
    out_grad = out_grad.transpose(1, 0, 2, 3).reshape(local_heads, all_rows, HEAD_DIM)
    following = passed_along(keys_values, "region", -1)
    reach = jnp.concatenate([keys_values, following], axis=2).reshape(
        2, local_heads, HEAD_DIM, 2 * latent
    )
    key_block = reach[0]
    value_block = reach[1]
    block_rows = min(512, all_rows)
    block_count = all_rows // block_rows

    def backward_block(totals, block_id):
        key_total, value_total = totals
        first_row = block_id * block_rows
        query_rows = lax.dynamic_slice_in_dim(queries, first_row, block_rows, 1)
        grad_rows = lax.dynamic_slice_in_dim(out_grad, first_row, block_rows, 1)
        scores = (
            jnp.einsum("hre,hek->hrk", query_rows, key_block, preferred_element_type=jnp.float32)
            * scale_back
        )
        row_max = jnp.max(scores, axis=2, keepdims=True)
        powers = jnp.exp(scores - row_max)
        attention = powers / jnp.sum(powers, axis=2, keepdims=True)
        rounded = attention.astype(jnp.bfloat16)
        prob_grad = jnp.einsum(
            "hre,hek->hrk", grad_rows, value_block, preferred_element_type=jnp.float32
        )
        row_dot = jnp.sum(attention * prob_grad, axis=2, keepdims=True)
        score_grad = (attention * (prob_grad - row_dot)).astype(jnp.bfloat16)
        query_grad = jnp.einsum(
            "hrk,hek->hre", score_grad, key_block, preferred_element_type=jnp.float32
        )
        query_grad = (query_grad * scale_back).astype(jnp.bfloat16)
        key_total = key_total + jnp.einsum(
            "hre,hrk->hek", query_rows, score_grad, preferred_element_type=jnp.float32
        )
        value_total = value_total + jnp.einsum(
            "hre,hrk->hek", grad_rows, rounded, preferred_element_type=jnp.float32
        )
        return ((key_total, value_total), query_grad)

    zero_grad = jnp.zeros((local_heads, HEAD_DIM, 2 * latent), jnp.float32)
    (key_total, value_total), grad_blocks = lax.scan(
        backward_block, (zero_grad, zero_grad), jnp.arange(block_count)
    )
    reach_grad = jnp.stack([key_total * scale_back, value_total]).reshape(
        2, local_heads * HEAD_DIM, 2 * latent
    )
    received = passed_along(reach_grad[:, :, latent:].astype(jnp.bfloat16), "region", 1).astype(
        jnp.float32
    )
    pair_grad = reach_grad[:, :, :latent] + received
    query_grad = grad_blocks.transpose(1, 0, 2, 3).reshape(local_heads, all_rows, HEAD_DIM)
    partial_grad = jnp.einsum(
        "hre,rf->hef", query_grad, feature_rows, preferred_element_type=jnp.float32
    )
    summed = lax.psum(partial_grad.reshape(local_heads * HEAD_DIM, width), "region")
    projection_grad = summed / regions
    return (pair_grad, projection_grad)


def solution(mesh):
    in_specs = (
        P("region", None, None, None),
        P("region", None, "mp", None),
        P(None, "mp", "region"),
        P("mp", None),
        P(),
    )
    out_specs = (P(None, "mp", "region"), P("mp", None))
    return jax.shard_map(
        per_device, mesh=mesh, in_specs=in_specs, out_specs=out_specs, check_vma=False
    )
```

profile of v0, /device:TPU:1, one launch (start us, length us, event | category | flops | bytes accessed | tf_op | source)
XLA Modules:
  0.0 521.8 jit_solution(607249014702080415)
XLA Ops:
  0.6 1.4 copy.18
  2.5 2.2 reduce.10
  4.9 71.5 %all_to_all.8 = bf16[64,2,1024]{2,1,0:T(2,128)(2,1)S(1)} all-to-all(bf16[64,2,1024]{2,1,0:T(2,128)(2,1)S(1)} %reshape.154), channel_id=1, replica_groups=mesh['region'=64,'mp'=16] {'region'}, dimensions={0} | all-to-all | bytes 524288 | tf_op jit(solution)/shard_map/all_to_all | solution.py:28
  76.4 6.5 %all-to-all-start = ((bf16[1,64,64,256]{3,2,0,1:T(8,128)(2,1)}), bf16[1,64,64,256]{3,2,0,1:T(8,128)(2,1)S(1)}, u32[]{:S(2)}, u32[]{:S(2)}) async-start(bf16[1,64,64,256]{3,2,0,1:T(8,128)(2,1)} %bitcast.99), calls=%async_computation | async-start | bytes 4194304 | tf_op jit(solution)/shard_map/all_to_all | solution.py:27
  83.8 177.6 %collective-permute-done = bf16[2,32,512]{2,1,0:T(8,128)(2,1)S(1)} collective-permute-done((bf16[2,32,512]{2,1,0:T(8,128)(2,1)S(1)}, bf16[2,32,512]{2,1,0:T(8,128)(2,1)S(1)}, u32[]{:S(2)}, u32[]{:S(2)}) %collective-permute-start) | collective-permute-done | bytes 65568 | tf_op jit(solution)/shard_map/ppermute | solution.py:13
  261.4 0.6 fusion.27
  262.3 2.1 bitcast_reduce_fusion
  264.5 1.9 reshape.145
  266.3 2.9 broadcast_select_fusion
  269.2 10.6 %all-to-all-done = bf16[1,64,64,256]{3,2,0,1:T(8,128)(2,1)S(1)} async-done(((bf16[1,64,64,256]{3,2,0,1:T(8,128)(2,1)}), bf16[1,64,64,256]{3,2,0,1:T(8,128)(2,1)S(1)}, u32[]{:S(2)}, u32[]{:S(2)}) %all-to-all-start) | async-done | bytes 2097184 | tf_op jit(solution)/shard_map/all_to_all | solution.py:27
  279.9 0.7 fusion.26
  280.6 0.6 copy-done.1
  281.2 55.0 %while.15 = (s32[]{:T(128)}, f32[1,32,1024]{2,1,0:T(8,128)S(1)}, f32[1,32,1024]{2,1,0:T(8,128)S(1)}, bf16[8,1,512,32]{2,3,1,0:T(8,128)(2,1)S(1)}, s32[8]{0:T(128...) while((s32[]{:T(128)}, f32[1,32,1024]{2,1,0:T(8,128)S(1)}, ...), condition=%wide.region_4.5_spmd.clone, body=%wide.region_0.4_spmd.clone.sunk | while | flops 178420224 | bytes 18929876 | solution.py:79
  283.5 1.6 fusion.53
  285.1 1.6 multiply_reduce_fusion.5
  286.7 0.6 multiply_convert_fusion.2
  288.1 0.6 dynamic_slice.51
  290.4 1.6 fusion.53
  292.0 1.6 multiply_reduce_fusion.5
  293.6 0.6 multiply_convert_fusion.2
  295.0 0.6 dynamic_slice.51
  297.3 1.6 fusion.53
  298.8 1.6 multiply_reduce_fusion.5
  300.4 0.6 multiply_convert_fusion.2
  304.1 1.6 fusion.53
  305.7 1.6 multiply_reduce_fusion.5
  307.3 0.6 multiply_convert_fusion.2
  308.7 0.6 dynamic_slice.51
  311.0 1.6 fusion.53
  312.6 1.6 multiply_reduce_fusion.5
  314.2 0.6 multiply_convert_fusion.2
  315.6 0.6 dynamic_slice.51
  317.9 1.6 fusion.53
  319.4 1.6 multiply_reduce_fusion.5
  321.1 0.6 multiply_convert_fusion.2
  322.4 0.6 dynamic_slice.51
  324.7 1.6 fusion.53
  326.3 1.6 multiply_reduce_fusion.5
  327.9 0.6 multiply_convert_fusion.2
  329.3 0.6 dynamic_slice.51
  331.6 1.6 fusion.53
  333.2 1.6 multiply_reduce_fusion.5
  334.8 0.6 multiply_convert_fusion.2
  336.2 1.2 collective-permute-start.1
  337.5 2.1 fusion.28
  339.5 181.0 %psum.7 = f32[32,256]{1,0:T(8,128)S(1)} all-reduce(f32[32,256]{1,0:T(8,128)S(1)} %fusion.28), channel_id=1, replica_groups=mesh['region'=64,'mp'=16] {'region'}, use_global_device_ids=true, to_apply=%region_5.6 | all-reduce | flops 8192 | bytes 65536 | tf_op jit(solution)/shard_map/psum | solution.py:93
  520.5 0.6 broadcast_multiply_fusion
  521.1 0.7 slice_add_fusion
  (63 shorter events, 17.4 us)
Async XLA Ops:
  0.6 82.8 %copy-start = (s32[64,64]{1,0:T(8,128)S(1)}, s32[64,64]{1,0:T(8,128)}, u32[]{:S(2)}) copy-start(s32[64,64]{1,0:T(8,128)} %param.11) | copy-start | bytes 49156
  76.4 6.5 %copy-start.3 = (bf16[2,32,512]{2,1,0:T(8,128)(2,1)S(1)}, bf16[2,32,512]{2,1,0:T(8,128)(2,1)}, u32[]{:S(2)}) copy-start(bf16[2,32,512]{2,1,0:T(8,128)(2,1)} %param.9) | copy-start | bytes 196612
  76.4 203.5 %all-to-all-start = ((bf16[1,64,64,256]{3,2,0,1:T(8,128)(2,1)}), bf16[1,64,64,256]{3,2,0,1:T(8,128)(2,1)S(1)}, u32[]{:S(2)}, u32[]{:S(2)}) async-start(bf16[1,64,64,256]{3,2,0,1:T(8,128)(2,1)} %bitcast.99), calls=%async_computation | async-start | bytes 4194304 | tf_op jit(solution)/shard_map/all_to_all | solution.py:27
  82.9 178.6 %collective-permute-start = (bf16[2,32,512]{2,1,0:T(8,128)(2,1)S(1)}, bf16[2,32,512]{2,1,0:T(8,128)(2,1)S(1)}, u32[]{:S(2)}, u32[]{:S(2)}) collective-permute-start(bf16[2,32,512]{2,1,0:T(8,128)(2,1)S(1)} %copy-done.3), channel_id=1, source_target_pairs={{0,1008},{16,0},{32,16},{48,32},{64,48},{80,64},{96,80},{112,96},{... | collective-permute-start | bytes 196616 | tf_op jit(solution)/shard_map/ppermute | solution.py:13
  262.3 17.6 %copy-start.5 = (bf16[32,256]{1,0:T(8,128)(2,1)S(1)}, bf16[32,256]{1,0:T(8,128)(2,1)}, u32[]{:S(2)}) copy-start(bf16[32,256]{1,0:T(8,128)(2,1)} %param.10) | copy-start | bytes 49156
  269.2 11.4 %copy-start.2 = (bf16[8,1,512,32]{2,3,1,0:T(8,128)(2,1)S(1)}, bf16[8,1,512,32]{2,3,1,0:T(8,128)(2,1)}, u32[]{:S(2)}) copy-start(bf16[8,1,512,32]{2,3,1,0:T(8,128)(2,1)} %custom-call.3) | copy-start | bytes 786436
  269.2 11.4 %copy-start.4 = (bf16[1,32,1024]{2,1,0:T(8,128)(2,1)S(1)}, bf16[1,32,1024]{2,1,0:T(8,128)(2,1)}, u32[]{:S(2)}) copy-start(bf16[1,32,1024]{2,1,0:T(8,128)(2,1)} %get-tuple-element.206) | copy-start | bytes 196612
  279.9 1.4 copy-start.1
  336.2 184.9 %collective-permute-start.1 = (bf16[2,32,512]{2,1,0:T(8,128)(2,1)S(1)}, bf16[2,32,512]{2,1,0:T(8,128)(2,1)S(1)}, u32[]{:S(2)}, u32[]{:S(2)}) collective-permute-start(bf16[2,32,512]{2,1,0:T(8,128)(2,1)S(1)} %slice.25), channel_id=1, source_target_pairs={{0,16},{16,32},{32,48},{48,64},{64,80},{80,96},{96,112},{112,128},... | collective-permute-start | bytes 196616 | tf_op jit(solution)/shard_map/ppermute | solution.py:13
where the time goes:
time: 525 us; the launch traced here: 522 us
  blocking collectives  252 us (48%)
  waiting for transfers between devices  188 us (36%)
  matrix products  38.4 us (7%)
  other arithmetic  15.5 us (3%)
  local copies, waits for them, and re-layouts  12.5 us (2%)
  starting transfers between devices  8.28 us (2%)
  loops' own time  5.55 us (1%)
    psum x1, blocking collectives, per_device(): lax.psum(partial_grad.reshape(local_heads * HEAD_DIM, width), 'region')  181 us
    ppermute x2, waiting for transfers between devices, passed_along(): lax.ppermute(array, axis, [(i, (i + by) % peers) for i in range(peers)])  178 us
    all_to_all x1, blocking collectives, per_device(): lax.all_to_all(cotangent, 'region', split_axis=1, concat_axis=0, tiled=True)  71.5 us
    dot_general x8, matrix products, backward_block(): jnp.einsum('hre,hek->hrk', grad_rows, value_block, preferred_element_type...  13 us
    dot_general x8, matrix products, backward_block(): jnp.einsum('hre,hrk->hek', grad_rows, rounded, preferred_element_type=jnp...  12.5 us
    all_to_all x1, waiting for transfers between devices, per_device(): lax.all_to_all(observations, 'region', split_axis=1, concat_axis=0, tiled...  10.6 us
  transfers between devices with their start and end apart: 3, of which 2 were waited for; matrix products, arithmetic and copies ran while one was open for 2% of the time, Pallas kernels for 0%

commit v1 on v0

v1 whole, which is shorter than its diff:
```python
import functools
import math

import jax
import jax.numpy as jnp
from jax import lax
from jax.experimental import pallas as pl
from jax.experimental.pallas import tpu as pltpu
from jax.sharding import PartitionSpec as P

HEAD_DIM = 32
MESH = pl.DeviceIdType.MESH
F32 = jnp.float32
BF16 = jnp.bfloat16


def slot_of(source, here, chips):
    away = (source // 2 - here // 2 + chips) % chips
    half = away // (chips // 2)
    block = (away * (1 - half) + (chips - away) * half) % (chips // 2)
    return block * 4 + half * 2 + source % 2


def kernel(
    regions,
    columns,
    counts_ref,
    obs_hbm,
    cot_hbm,
    kv_ref,
    weight_ref,
    pair_ref,
    proj_ref,
    obs_buf,
    cot_buf,
    kv_next,
    key_rows,
    value_rows,
    key_cols,
    key_acc,
    value_acc,
    proj_acc,
    edge_out,
    edge_in,
    part_out,
    part_in,
    group_in,
    final_in,
    obs_recv,
    cot_recv,
    obs_send,
    relay_send,
    cot_send,
    own_sem,
    kv_sems,
    edge_sems,
    part_sems,
    group_sems,
    final_sems,
):
    chips = regions // 2
    me = lax.axis_index("region")
    col = lax.axis_index("mp")
    my_chip = me // 2
    my_core = me % 2
    latent = kv_ref.shape[2]
    shares = regions // columns
    blocks = regions // 4

    barrier = pltpu.get_barrier_semaphore()

    def greet_region(i, carry):
        peer = (me + i) % regions
        pl.semaphore_signal(barrier, inc=1, device_id=(peer, col), device_id_type=MESH)
        return carry

    def greet_column(i, carry):
        peer = (col + i) % columns
        pl.semaphore_signal(barrier, inc=1, device_id=(me, peer), device_id_type=MESH)
        return carry

    lax.fori_loop(1, regions, greet_region, 0)
    lax.fori_loop(1, columns, greet_column, 0)
    own_slot = my_core
    own_obs = pltpu.make_async_copy(obs_hbm.at[me], obs_buf.at[own_slot], obs_recv.at[own_slot])
    own_cot = pltpu.make_async_copy(cot_hbm.at[me], cot_buf.at[own_slot], cot_recv.at[own_slot])
    own_obs.start()
    own_cot.start()

    key_cols[...] = jnp.concatenate([kv_ref[0], kv_ref[0]], axis=1)
    pl.semaphore_wait(barrier, regions - 1 + columns - 1)

    kv_copy = pltpu.make_async_remote_copy(
        src_ref=kv_ref,
        dst_ref=kv_next,
        send_sem=kv_sems.at[0],
        recv_sem=kv_sems.at[1],
        device_id=((me + regions - 1) % regions, col),
        device_id_type=MESH,
    )
    kv_copy.start()

    first_share = (col - me + regions * columns) % columns

    def obs_copy(t):
        peer = first_share + columns * t
        slot = slot_of(me, peer, chips)
        return peer, pltpu.make_async_remote_copy(
            src_ref=obs_hbm.at[peer],
            dst_ref=obs_buf.at[slot],
            send_sem=obs_send.at[t],
            recv_sem=obs_recv.at[slot],
            device_id=(peer, col),
            device_id_type=MESH,
        )

    for t in range(shares):
        peer, copy = obs_copy(t)

        @pl.when(peer != me)
        def _():
            copy.start()

    def cot_copy(chip, core):
        peer = (chip % chips) * 2 + core
        slot = slot_of(me, peer, chips)
        return pltpu.make_async_remote_copy(
            src_ref=cot_hbm.at[peer],
            dst_ref=cot_buf.at[slot],
            send_sem=cot_send,
            recv_sem=cot_recv.at[slot],
            device_id=(peer, col),
            device_id_type=MESH,
        )

    cot_copy(my_chip, 1 - my_core).start()

    def send_at_distance(k, carry):
        for core in range(2):
            cot_copy(my_chip + k, core).start()
            cot_copy(my_chip + chips - k, core).start()
        return carry

    lax.fori_loop(1, chips // 2, send_at_distance, 0)
    for core in range(2):
        cot_copy(my_chip + chips // 2, core).start()

    def wait_obs(slot):
        pltpu.make_async_copy(obs_hbm.at[0], obs_buf.at[slot], obs_recv.at[slot]).wait()

    def wait_cot(slot):
        pltpu.make_async_copy(cot_hbm.at[0], cot_buf.at[slot], cot_recv.at[slot]).wait()

    for t in range(shares):
        source = first_share + columns * t
        slot = slot_of(source, me, chips)

        @pl.when(source != me)
        def _():
            wait_obs(slot)

            def relay(i, carry):
                pltpu.make_async_remote_copy(
                    src_ref=obs_buf.at[slot],
                    dst_ref=obs_buf.at[slot],
                    send_sem=relay_send.at[t],
                    recv_sem=obs_recv.at[slot],
                    device_id=(me, (col + i) % columns),
                    device_id_type=MESH,
                ).start()
                return carry

            lax.fori_loop(1, columns, relay, 0)

    kv_copy.wait_recv()
    key_cols[:, latent:] = kv_next[0]
    key_rows[...] = jnp.transpose(key_cols[...].astype(F32)).astype(BF16)
    values = jnp.concatenate([kv_ref[1], kv_next[1]], axis=1)
    values = jnp.transpose(values.astype(F32)).astype(BF16)
    value_rows[...] = jnp.concatenate([values] * 4, axis=1)
    key_acc[...] = jnp.zeros_like(key_acc)
    value_acc[...] = jnp.zeros_like(value_acc)
    proj_acc[...] = jnp.zeros_like(proj_acc)

    rows = 4 * obs_buf.shape[1]
    slots = obs_buf.shape[1]
    packed = cot_buf.shape[1]
    scale_back = 1.0 / math.sqrt(HEAD_DIM)
    power_scale = scale_back * math.log2(math.e)
    spread = (
        lax.broadcasted_iota(jnp.int32, (rows, 4 * packed), 0) // 4
        == lax.broadcasted_iota(jnp.int32, (rows, 4 * packed), 1)
    ).astype(F32).astype(BF16)

    def source_at(block, part):
        half = part // 2
        away = jnp.where(block == 0, half * (chips // 2), jnp.where(half == 0, block, chips - block))
        return ((my_chip + away) % chips) * 2 + part % 2

    def attend(step, carry):
        block = (step + 1) % blocks
        for part in range(4):
            slot = block * 4 + part
            source = source_at(block, part)

            if part < 2:
                wait_cot(slot)

                @pl.when(jnp.logical_or((source + me) % columns != col, source == me))
                def _():
                    wait_obs(slot)
            else:
                wait_cot(slot)

                @pl.when((source + me) % columns != col)
                def _():
                    wait_obs(slot)

        obs = obs_buf[pl.ds(block * 4, 4)].reshape(rows, obs_buf.shape[2])
        cot = cot_buf[pl.ds(block * 4, 4)].reshape(4 * packed, cot_buf.shape[2])
        query = lax.dot_general(
            obs, weight_ref[...], (((1,), (1,)), ((), ())), preferred_element_type=F32
        ).astype(BF16)
        grads = lax.dot_general(
            spread, cot, (((1,), (0,)), ((), ())), preferred_element_type=F32
        )
        row = lax.broadcasted_iota(jnp.int32, (slots, grads.shape[1]), 0)
        lane = lax.broadcasted_iota(jnp.int32, (slots, grads.shape[1]), 1)
        band = lane // HEAD_DIM == row % 4
        pieces = []
        for part in range(4):
            live = counts_ref[source_at(block, part), me]
            keep = jnp.logical_and(band, row < live)
            piece = grads[part * slots : (part + 1) * slots]
            pieces.append(jnp.where(keep, piece, 0.0))
        grads = jnp.concatenate(pieces, axis=0).astype(BF16)

        scores = lax.dot_general(
            key_rows[...], query, (((1,), (1,)), ((), ())), preferred_element_type=F32
        )
        top = jnp.max(scores, axis=0, keepdims=True)
        powers = jnp.exp2((scores - top) * power_scale)
        attention = powers * (1.0 / jnp.sum(powers, axis=0, keepdims=True))
        prob_grad = lax.dot_general(
            value_rows[...], grads, (((1,), (1,)), ((), ())), preferred_element_type=F32
        )
        row_dot = jnp.sum(attention * prob_grad, axis=0, keepdims=True)
        score_grad = (attention * (prob_grad - row_dot)).astype(BF16)
        key_acc[...] += jnp.dot(score_grad, query, preferred_element_type=F32)
        value_acc[...] += jnp.dot(attention.astype(BF16), grads, preferred_element_type=F32)
        query_grad = jnp.dot(key_cols[...], score_grad, preferred_element_type=F32)
        query_grad = (query_grad * scale_back).astype(BF16)
        proj_acc[...] += jnp.dot(query_grad, obs, preferred_element_type=F32)
        return carry

    lax.fori_loop(0, blocks, attend, 0)

    group = me // 8
    member = me % 8
    groups = regions // 8
    tiles = [(r, c) for r in range(0, proj_acc.shape[0], 8) for c in range(0, proj_acc.shape[1], 128)]
    for index, (r, c) in enumerate(tiles):
        part_out[index] = proj_acc[r : r + 8, c : c + 128]

    def part_copy(i):
        peer = (member + i) % 8
        return pltpu.make_async_remote_copy(
            src_ref=part_out.at[peer],
            dst_ref=part_in.at[i - 1],
            send_sem=part_sems.at[0, i - 1],
            recv_sem=part_sems.at[1, i - 1],
            device_id=(group * 8 + peer, col),
            device_id_type=MESH,
        )

    for i in range(1, 8):
        part_copy(i).start()

    key_grad = jnp.transpose(key_acc[...]) * scale_back
    value_grad = jnp.transpose(value_acc[...])
    value_grad = (value_grad[:HEAD_DIM] + value_grad[HEAD_DIM : 2 * HEAD_DIM]) + (
        value_grad[2 * HEAD_DIM : 3 * HEAD_DIM] + value_grad[3 * HEAD_DIM :]
    )
    edge_out[0] = key_grad[:, latent:].astype(BF16)
    edge_out[1] = value_grad[:, latent:].astype(BF16)
    edge_copy = pltpu.make_async_remote_copy(
        src_ref=edge_out,
        dst_ref=edge_in,
        send_sem=edge_sems.at[0],
        recv_sem=edge_sems.at[1],
        device_id=((me + 1) % regions, col),
        device_id_type=MESH,
    )
    edge_copy.start()
    pair_ref[0] = key_grad[:, :latent]
    pair_ref[1] = value_grad[:, :latent]

    for i in range(1, 8):
        part_copy(i).wait_recv()
    total = part_out[member]
    for i in range(1, 8):
        total = total + part_in[i - 1]
    group_in[group] = total

    def group_copy(i):
        peer = (group + i) % groups
        return pltpu.make_async_remote_copy(
            src_ref=group_in.at[group],
            dst_ref=group_in.at[group],
            send_sem=group_sems.at[0, i - 1],
            recv_sem=group_sems.at[1, group],
            device_id=(peer * 8 + member, col),
            device_id_type=MESH,
        )

    for i in range(1, groups):
        group_copy(i).start()

    edge_copy.wait_recv()
    pair_ref[...] += edge_in[...].astype(F32)

    for i in range(1, groups):
        peer = (group + i) % groups
        pltpu.make_async_copy(
            group_in.at[peer], group_in.at[peer], group_sems.at[1, peer]
        ).wait()
    total = group_in[0]
    for index in range(1, groups):
        total = total + group_in[index]
    final_in[member] = total * (1.0 / regions)

    def final_copy(i):
        peer = (member + i) % 8
        return pltpu.make_async_remote_copy(
            src_ref=final_in.at[member],
            dst_ref=final_in.at[member],
            send_sem=final_sems.at[0, i - 1],
            recv_sem=final_sems.at[1, member],
            device_id=(group * 8 + peer, col),
            device_id_type=MESH,
        )

    for i in range(1, 8):
        final_copy(i).start()
    for i in range(1, 8):
        peer = (member + i) % 8
        pltpu.make_async_copy(
            final_in.at[peer], final_in.at[peer], final_sems.at[1, peer]
        ).wait()
    for index, (r, c) in enumerate(tiles):
        proj_ref[r : r + 8, c : c + 128] = final_in[index]

    kv_copy.wait_send()
    edge_copy.wait_send()
    for t in range(shares):
        peer, copy = obs_copy(t)

        @pl.when(peer != me)
        def _():
            copy.wait_send()
            many = pl.ds(0, columns - 1)
            pltpu.make_async_copy(obs_buf.at[many], obs_buf.at[many], relay_send.at[t]).wait()

    many = pl.ds(0, regions - 1)
    pltpu.make_async_copy(cot_buf.at[many], cot_buf.at[many], cot_send).wait()
    for i in range(1, 8):
        part_copy(i).wait_send()
        final_copy(i).wait_send()
    for i in range(1, groups):
        group_copy(i).wait_send()


def per_device(observations, cotangent, keys_values, query_weight, counts):
    regions = lax.axis_size("region")
    columns = lax.axis_size("mp")
    capacity = observations.shape[2]
    width = observations.shape[3]
    latent = keys_values.shape[2]
    reach = 2 * latent
    packed = capacity * HEAD_DIM // 128
    cot = cotangent.reshape(regions, packed, 128)
    vmem = pl.BlockSpec(memory_space=pltpu.VMEM)
    hbm = pl.BlockSpec(memory_space=pl.ANY)
    dma = pltpu.SemaphoreType.DMA
    groups = regions // 8
    pair_grad, projection_grad = pl.pallas_call(
        functools.partial(kernel, regions, columns),
        name="region_backward",
        out_shape=(
            jax.ShapeDtypeStruct((2, HEAD_DIM, latent), F32),
            jax.ShapeDtypeStruct((HEAD_DIM, width), F32),
        ),
        in_specs=[pl.BlockSpec(memory_space=pltpu.SMEM), hbm, hbm, vmem, vmem],
        out_specs=(vmem, vmem),
        scratch_shapes=[
            pltpu.VMEM((regions, capacity, width), BF16),
            pltpu.VMEM((regions, packed, 128), BF16),
            pltpu.VMEM((2, HEAD_DIM, latent), BF16),
            pltpu.VMEM((reach, HEAD_DIM), BF16),
            pltpu.VMEM((reach, 4 * HEAD_DIM), BF16),
            pltpu.VMEM((HEAD_DIM, reach), BF16),
            pltpu.VMEM((reach, HEAD_DIM), F32),
            pltpu.VMEM((reach, 4 * HEAD_DIM), F32),
            pltpu.VMEM((HEAD_DIM, width), F32),
            pltpu.VMEM((2, HEAD_DIM, latent), BF16),
            pltpu.VMEM((2, HEAD_DIM, latent), BF16),
            pltpu.VMEM((8, 8, 128), F32),
            pltpu.VMEM((7, 8, 128), F32),
            pltpu.VMEM((groups, 8, 128), F32),
            pltpu.VMEM((8, 8, 128), F32),
            dma((regions,)),
            dma((regions,)),
            dma((regions // columns,)),
            dma((regions // columns,)),
            dma,
            dma((1,)),
            dma((2,)),
            dma((2,)),
            dma((2, 7)),
            dma((2, groups)),
            dma((2, 8)),
        ],
        compiler_params=pltpu.CompilerParams(collective_id=0, has_side_effects=True),
    )(counts, observations[0], cot, keys_values, query_weight)
    return (pair_grad, projection_grad)


def solution(mesh):
    in_specs = (
        P("region", None, None, None),
        P("region", None, "mp", None),
        P(None, "mp", "region"),
        P("mp", None),
        P(),
    )
    out_specs = (P(None, "mp", "region"), P("mp", None))
    return jax.shard_map(
        per_device, mesh=mesh, in_specs=in_specs, out_specs=out_specs, check_vma=False
    )
```

time: 525 us -> 125 us (0.24)
  blocking collectives: 252 us -> 0 us
  waiting for transfers between devices: 188 us -> 0 us
  Pallas kernels: 0 us -> 119 us
  matrix products: 38.4 us -> 0 us
  other arithmetic: 15.5 us -> 0 us
  starting transfers between devices: 8.28 us -> 0 us
  local copies, waits for them, and re-layouts: 12.5 us -> 4.63 us
  loops' own time: 5.55 us -> 0 us
    psum x1 -> x0, blocking collectives: 181 us -> none  [per_device(): lax.psum(partial_grad.reshape(local_heads * HEAD_DIM, width), 'region')]
    ppermute x2 -> x0, waiting for transfers between devices: 178 us -> none  [passed_along(): lax.ppermute(array, axis, [(i, (i + by) % peers) for i in range(peers)])]
    pallas_call x0 -> x1, Pallas kernels: none -> 119 us  [per_device(): pl.pallas_call(functools.partial(kernel, regions, columns), name='region_...]
    all_to_all x1 -> x0, blocking collectives: 71.5 us -> none  [per_device(): lax.all_to_all(cotangent, 'region', split_axis=1, concat_axis=0, tiled=True)]
    dot_general x42 -> x0, matrix products: 38.4 us -> none  [the longest x8 13 us: backward_block(): jnp.einsum('hre,hek->hrk', grad_rows, value_block, preferred_element_type...]
    all_to_all x1 -> x0, waiting for transfers between devices: 10.6 us -> none  [per_device(): lax.all_to_all(observations, 'region', split_axis=1, concat_axis=0, tiled...]
    all_to_all x1 -> x0, starting transfers between devices: 6.48 us -> none  [per_device(): lax.all_to_all(observations, 'region', split_axis=1, concat_axis=0, tiled...]
    another operation x1 -> x0, loops' own time: 5.55 us -> none  [per_device(): lax.scan(backward_block, (zero_grad, zero_grad), jnp.arange(block_count))]
  transfers between devices with their start and end apart: 3 -> 0, of which waited for: 2 -> 0; matrix products, arithmetic and copies ran while one was open for 2% -> 0% of each run, Pallas kernels for 0% -> 0%
where the time goes in v1:
time: 125 us
  Pallas kernels  119 us (95%)
  local copies, waits for them, and re-layouts  4.63 us (4%)
    pallas_call x1, Pallas kernels, per_device(): pl.pallas_call(functools.partial(kernel, regions, columns), name='region_...  119 us
    unnamed x3, local copies, waits for them, and re-layouts  4.63 us

profile of v1, /device:TPU:1, one launch (start us, length us, event | category | flops | bytes accessed | tf_op | source)
XLA Modules:
  0.0 124.6 jit_solution(16887862954162706084)
XLA Ops:
  0.6 1.7 %copy.7 = bf16[8,8,16,128]{3,2,1,0:T(8,128)(2,1)} copy(bf16[8,8,16,128]{3,1,2,0:T(8,128)(2,1)} %bitcast.8) | data formatting | bytes 524288
  2.3 119.3 %region_backward.1 = (f32[2,32,512]{2,1,0:T(8,128)}, f32[32,256]{1,0:T(8,128)}) custom-call(s32[64,64]{1,0:T(8,128)} %counts_ref.1, bf16[64,64,256]{2,1,0:T(8,128)(2,1)} %bitcast.6, bf16[64,16,128]{2,1,0:T(8,128)(2,1)} %bitcast.7, bf16[2,32,512]{2,1,0:T(8,128)(2,1)} %kv_ref.1, bf16[32,256]{1,0:T(8,128)(2,1)} %weight_ref.1), custom_call_target="tpu_custom_call" | custom-call | tf_op jit(solution)/shard_map/region_backward/pallas_call | solution.py:386
  121.6 1.6 %copy.10 = f32[2,32,512]{2,1,0:T(8,128)} copy(f32[2,32,512]{2,1,0:T(8,128)} %get-tuple-element.4) | data formatting | bytes 262144
  123.2 1.4 %copy.11 = f32[32,256]{1,0:T(8,128)} copy(f32[32,256]{1,0:T(8,128)} %get-tuple-element.5) | data formatting | bytes 65536

commit v2 on v1

v2 whole, which is shorter than its diff:
```python
import functools
import math

import jax
import jax.numpy as jnp
from jax import lax
from jax.experimental import pallas as pl
from jax.experimental.pallas import tpu as pltpu
from jax.sharding import PartitionSpec as P

HEAD_DIM = 32
FIRST_LAG = 3
SECOND_LAG = 6
MESH = pl.DeviceIdType.MESH
F32 = jnp.float32
BF16 = jnp.bfloat16


def slot_of(source, here, chips):
    away = (source // 2 - here // 2 + chips) % chips
    half = away // (chips // 2)
    block = (away * (1 - half) + (chips - away) * half) % (chips // 2)
    return block * 4 + half * 2 + source % 2


def kernel(
    regions,
    columns,
    counts_ref,
    obs_hbm,
    cot_hbm,
    kv_ref,
    weight_ref,
    pair_ref,
    proj_ref,
    obs_buf,
    cot_buf,
    kv_next,
    reach_rows,
    reach_cols,
    weight_rows,
    reach_acc,
    proj_acc,
    scores_buf,
    grads_buf,
    rows_buf,
    top_buf,
    edge_out,
    edge_in,
    part_out,
    part_in,
    group_in,
    final_in,
    obs_recv,
    cot_recv,
    obs_send,
    relay_send,
    cot_send,
    own_sem,
    kv_sems,
    edge_sems,
    part_sems,
    group_sems,
    final_sems,
):
    chips = regions // 2
    me = lax.axis_index("region")
    col = lax.axis_index("mp")
    my_chip = me // 2
    my_core = me % 2
    latent = kv_ref.shape[2]
    blocks = regions // 4

    across = 4
    def along_x(i):
        return (col // across) * across + (col % across + i) % across

    def along_y(i):
        return (col + i * across) % columns

    barrier = pltpu.get_barrier_semaphore()

    def tell(sem, region, column):
        pl.semaphore_signal(sem, inc=1, device_id=(region, column), device_id_type=MESH)

    def greet_region(i, carry):
        tell(barrier, (me + i) % regions, col)
        return carry

    lax.fori_loop(1, regions, greet_region, 0)
    for i in range(1, across):
        tell(barrier, me, along_x(i))
        tell(barrier, me, along_y(i))
    own_slot = my_core
    own_obs = pltpu.make_async_copy(obs_hbm.at[me], obs_buf.at[own_slot], obs_recv.at[own_slot])
    own_cot = pltpu.make_async_copy(cot_hbm.at[me], cot_buf.at[own_slot], cot_recv.at[own_slot])
    own_obs.start()
    own_cot.start()

    reach_cols[:HEAD_DIM, :latent] = kv_ref[0]
    reach_cols[HEAD_DIM:, :latent] = kv_ref[1]
    weight_rows[:HEAD_DIM] = weight_ref[...]
    weight_rows[HEAD_DIM:] = jnp.zeros_like(weight_ref)
    reach_acc[...] = jnp.zeros_like(reach_acc)
    proj_acc[...] = jnp.zeros_like(proj_acc)
    for ref in (*scores_buf, *grads_buf, *rows_buf, *top_buf):
        ref[...] = jnp.zeros_like(ref)
    pl.semaphore_wait(barrier, regions - 1 + 2 * (across - 1))
    kv_copy = pltpu.make_async_remote_copy(
        src_ref=kv_ref,
        dst_ref=kv_next,
        send_sem=kv_sems.at[0],
        recv_sem=kv_sems.at[1],
        device_id=((me + regions - 1) % regions, col),
        device_id_type=MESH,
    )

    def obs_copy(peer):
        slot = slot_of(me, peer, chips)
        return pltpu.make_async_remote_copy(
            src_ref=obs_hbm.at[peer],
            dst_ref=obs_buf.at[slot],
            send_sem=obs_send.at[peer // columns],
            recv_sem=obs_recv.at[slot],
            device_id=(peer, col),
            device_id_type=MESH,
        )

    def cot_copy(chip, core):
        peer = (chip % chips) * 2 + core
        slot = slot_of(me, peer, chips)
        return pltpu.make_async_remote_copy(
            src_ref=cot_hbm.at[peer],
            dst_ref=cot_buf.at[slot],
            send_sem=cot_send,
            recv_sem=cot_recv.at[slot],
            device_id=(peer, col),
            device_id_type=MESH,
        )

    kv_copy.start()
    for t in range(regions // columns):
        peer = (col - me + regions * columns) % columns + columns * t

        @pl.when(peer != me)
        def _():
            obs_copy(peer).start()

    def send_at_distance(k, carry):
        for core in range(2):
            cot_copy(my_chip + k, core).start()
            cot_copy(my_chip + chips - k, core).start()
        return carry

    cot_copy(my_chip, 1 - my_core).start()
    lax.fori_loop(1, chips // 2, send_at_distance, 0)
    for core in range(2):
        cot_copy(my_chip + chips // 2, core).start()

    def wait_obs(slot):
        pltpu.make_async_copy(obs_hbm.at[0], obs_buf.at[slot], obs_recv.at[slot]).wait()

    def wait_cot(slot):
        pltpu.make_async_copy(cot_hbm.at[0], cot_buf.at[slot], cot_recv.at[slot]).wait()

    kv_copy.wait_recv()
    reach_cols[:HEAD_DIM, latent:] = kv_next[0]
    reach_cols[HEAD_DIM:, latent:] = kv_next[1]
    reach_rows[...] = jnp.transpose(reach_cols[...].astype(F32)).astype(BF16)

    rows = 4 * obs_buf.shape[1]
    slots = obs_buf.shape[1]
    packed = cot_buf.shape[1]
    scale_back = 1.0 / math.sqrt(HEAD_DIM)
    power_scale = scale_back * math.log2(math.e)
    spread = (
        lax.broadcasted_iota(jnp.int32, (rows, 4 * packed), 0) // 4
        == lax.broadcasted_iota(jnp.int32, (rows, 4 * packed), 1)
    ).astype(F32).astype(BF16)

    fold = (
        lax.broadcasted_iota(jnp.int32, (4 * HEAD_DIM, 2 * HEAD_DIM), 0) % HEAD_DIM + HEAD_DIM
        == lax.broadcasted_iota(jnp.int32, (4 * HEAD_DIM, 2 * HEAD_DIM), 1)
    ).astype(F32).astype(BF16)
    row = lax.broadcasted_iota(jnp.int32, (slots, 4 * HEAD_DIM), 0)
    lane = lax.broadcasted_iota(jnp.int32, (slots, 4 * HEAD_DIM), 1)
    band = lane // HEAD_DIM == row % 4
    chunk = 128
    chunks = 2 * latent // chunk

    def source_at(block, part):
        half = part // 2
        away = jnp.where(block == 0, half * (chips // 2), jnp.where(half == 0, block, chips - block))
        return ((my_chip + away) % chips) * 2 + part % 2

    def relay(slot, peer):
        pltpu.make_async_remote_copy(
            src_ref=obs_buf.at[slot],
            dst_ref=obs_buf.at[slot],
            send_sem=relay_send.at[slot],
            recv_sem=obs_recv.at[slot],
            device_id=(me, peer),
            device_id_type=MESH,
        ).start()

    def in_line(part, owner):
        if part < 2:
            return owner // across == col // across
        return owner % across == col % across

    def each_part(block):
        for part in range(4):
            source = source_at(block, part)
            yield part, block * 4 + part, source, (source + me) % columns

    def spread_first(block):
        for part, slot, source, owner in each_part(block):

            @pl.when(jnp.logical_and(owner == col, source != me))
            def _():
                wait_obs(slot)
                for i in range(1, across):
                    relay(slot, along_x(i) if part < 2 else along_y(i))

    def spread_second(block):
        for part, slot, source, owner in each_part(block):

            @pl.when(jnp.logical_and(in_line(part, owner), source != me))
            def _():
                @pl.when(owner != col)
                def _():
                    wait_obs(slot)

                for i in range(1, across):
                    relay(slot, along_y(i) if part < 2 else along_x(i))

    def arrived(block):
        for part, slot, source, owner in each_part(block):
            wait_cot(slot)

            @pl.when(jnp.logical_or(jnp.logical_not(in_line(part, owner)), source == me))
            def _():
                wait_obs(slot)

    def block_obs(block):
        return obs_buf[pl.ds(block * 4, 4)].reshape(rows, obs_buf.shape[2])

    def fold_rows(value):
        return value.reshape(chunk // 8, 8, rows)

    def compute(block, last, even):
        scores_now, scores_before = scores_buf[even], scores_buf[1 - even]
        grads_now, grads_before = grads_buf[1 - even], grads_buf[even]
        rows_ref = rows_buf[even]
        top = jnp.max(top_buf[1 - even][...], axis=0, keepdims=True)
        total = jnp.zeros((8, rows), F32)
        row_dot = jnp.zeros((8, rows), F32)
        query_grad = jnp.zeros((HEAD_DIM, rows), F32)
        for index in range(chunks):
            where = slice(index * chunk, (index + 1) * chunk)
            powers = jnp.exp2((scores_before[where, :rows] - top) * power_scale)
            scores_before[where, :rows] = powers
            total = total + jnp.sum(fold_rows(powers), axis=0)
            row_dot = row_dot + jnp.sum(fold_rows(powers * scores_before[where, rows:]), axis=0)
            reach_acc[where] += jnp.dot(
                grads_before[where], rows_ref[...], preferred_element_type=F32
            )
            if index % 2:
                pair = slice((index - 1) * chunk, (index + 1) * chunk)
                query_grad = query_grad + jnp.dot(
                    reach_cols[:HEAD_DIM, pair],
                    grads_before[pair, :rows],
                    preferred_element_type=F32,
                )
            if index == 1:
                cot = cot_buf[pl.ds(block * 4, 4)].reshape(4 * packed, cot_buf.shape[2])
                query = lax.dot_general(
                    block_obs(block),
                    weight_rows[...],
                    (((1,), (1,)), ((), ())),
                    preferred_element_type=F32,
                ).astype(BF16)
                wide = jnp.dot(spread, cot, preferred_element_type=F32)
                pieces = []
                for part in range(4):
                    live = counts_ref[source_at(block, part), me]
                    keep = jnp.logical_and(band, row < live)
                    pieces.append(jnp.where(keep, wide[part * slots : (part + 1) * slots], 0.0))
                wide = jnp.concatenate(pieces, axis=0).astype(BF16)
            if index == 4:
                grads = jnp.dot(wide, fold, preferred_element_type=F32).astype(BF16)
        rows_ref[:rows] = query
        rows_ref[rows:] = grads
        both = jnp.concatenate([query, grads], axis=0)
        inverse = 1.0 / jnp.sum(total, axis=0, keepdims=True)
        row_dot = jnp.sum(row_dot, axis=0, keepdims=True) * inverse
        query_grad = (query_grad * scale_back).astype(BF16)
        highest = None
        for index in range(chunks):
            where = slice(index * chunk, (index + 1) * chunk)
            products = lax.dot_general(
                reach_rows[where], both, (((1,), (1,)), ((), ())), preferred_element_type=F32
            )
            scores_now[where] = products
            here = jnp.max(fold_rows(products[:, :rows]), axis=0)
            highest = here if highest is None else jnp.maximum(highest, here)
            attention = scores_before[where, :rows] * inverse
            score_grad = attention * (scores_before[where, rows:] - row_dot)
            grads_now[where, :rows] = score_grad.astype(BF16)
            grads_now[where, rows:] = attention.astype(BF16)
            if index == 3:
                proj_acc[...] += jnp.dot(query_grad, block_obs(last), preferred_element_type=F32)
        top_buf[even][...] = highest

    def at(index):
        return (jnp.clip(index, 0, blocks - 1) + 1) % blocks

    def stage(step, even):
        @pl.when(step < blocks)
        def _():
            spread_first((step + 1) % blocks)

        @pl.when(jnp.logical_and(step >= FIRST_LAG, step < blocks + FIRST_LAG))
        def _():
            spread_second((step - FIRST_LAG + 1) % blocks)

        index = step - SECOND_LAG

        @pl.when(jnp.logical_and(index >= 0, index < blocks))
        def _():
            arrived(at(index))

        @pl.when(index >= 0)
        def _():
            compute(at(index), at(index - 2), even)

    def stages(pair, carry):
        for even in range(2):
            stage(pair * 2 + even, even)
        return carry

    lax.fori_loop(0, (blocks + 2 + SECOND_LAG) // 2, stages, 0)

    group = me // 8
    member = me % 8
    groups = regions // 8
    tiles = [(r, c) for r in range(0, proj_acc.shape[0], 8) for c in range(0, proj_acc.shape[1], 128)]
    for index, (r, c) in enumerate(tiles):
        part_out[index] = proj_acc[r : r + 8, c : c + 128]

    def part_copy(i):
        peer = (member + i) % 8
        return pltpu.make_async_remote_copy(
            src_ref=part_out.at[peer],
            dst_ref=part_in.at[i - 1],
            send_sem=part_sems.at[0, i - 1],
            recv_sem=part_sems.at[1, i - 1],
            device_id=(group * 8 + peer, col),
            device_id_type=MESH,
        )

    for i in range(1, 8):
        part_copy(i).start()

    reach_grad = jnp.transpose(reach_acc[...])
    key_grad = reach_grad[:HEAD_DIM] * scale_back
    value_grad = reach_grad[HEAD_DIM:]
    edge_out[0] = key_grad[:, latent:].astype(BF16)
    edge_out[1] = value_grad[:, latent:].astype(BF16)
    edge_copy = pltpu.make_async_remote_copy(
        src_ref=edge_out,
        dst_ref=edge_in,
        send_sem=edge_sems.at[0],
        recv_sem=edge_sems.at[1],
        device_id=((me + 1) % regions, col),
        device_id_type=MESH,
    )
    edge_copy.start()
    pair_ref[0] = key_grad[:, :latent]
    pair_ref[1] = value_grad[:, :latent]

    for i in range(1, 8):
        part_copy(i).wait_recv()
    total = part_out[member]
    for i in range(1, 8):
        total = total + part_in[i - 1]
    group_in[group] = total

    def group_copy(i):
        peer = (group + i) % groups
        return pltpu.make_async_remote_copy(
            src_ref=group_in.at[group],
            dst_ref=group_in.at[group],
            send_sem=group_sems.at[0, i - 1],
            recv_sem=group_sems.at[1, group],
            device_id=(peer * 8 + member, col),
            device_id_type=MESH,
        )

    for i in range(1, groups):
        group_copy(i).start()

    def sent_block(block, carry):
        for part, slot, source, owner in each_part(block):

            @pl.when(jnp.logical_and(owner == col, source != me))
            def _():
                obs_copy(source).wait_send()
                many = pl.ds(0, 2 * across - 2)
                pltpu.make_async_copy(obs_buf.at[many], obs_buf.at[many], relay_send.at[slot]).wait()

            @pl.when(
                jnp.logical_and(
                    jnp.logical_and(in_line(part, owner), owner != col), source != me
                )
            )
            def _():
                many = pl.ds(0, across - 1)
                pltpu.make_async_copy(obs_buf.at[many], obs_buf.at[many], relay_send.at[slot]).wait()

        return carry

    lax.fori_loop(0, blocks, sent_block, 0)
    edge_copy.wait_recv()
    pair_ref[...] += edge_in[...].astype(F32)

    for i in range(1, groups):
        peer = (group + i) % groups
        pltpu.make_async_copy(
            group_in.at[peer], group_in.at[peer], group_sems.at[1, peer]
        ).wait()
    total = group_in[0]
    for index in range(1, groups):
        total = total + group_in[index]
    final_in[member] = total * (1.0 / regions)

    def final_copy(i):
        peer = (member + i) % 8
        return pltpu.make_async_remote_copy(
            src_ref=final_in.at[member],
            dst_ref=final_in.at[member],
            send_sem=final_sems.at[0, i - 1],
            recv_sem=final_sems.at[1, member],
            device_id=(group * 8 + peer, col),
            device_id_type=MESH,
        )

    for i in range(1, 8):
        final_copy(i).start()
    for i in range(1, 8):
        peer = (member + i) % 8
        pltpu.make_async_copy(
            final_in.at[peer], final_in.at[peer], final_sems.at[1, peer]
        ).wait()
    for index, (r, c) in enumerate(tiles):
        proj_ref[r : r + 8, c : c + 128] = final_in[index]

    kv_copy.wait_send()
    edge_copy.wait_send()
    many = pl.ds(0, regions - 1)
    pltpu.make_async_copy(cot_buf.at[many], cot_buf.at[many], cot_send).wait()
    for i in range(1, 8):
        part_copy(i).wait_send()
        final_copy(i).wait_send()
    for i in range(1, groups):
        group_copy(i).wait_send()


def per_device(observations, cotangent, keys_values, query_weight, counts):
    regions = lax.axis_size("region")
    columns = lax.axis_size("mp")
    capacity = observations.shape[2]
    width = observations.shape[3]
    latent = keys_values.shape[2]
    reach = 2 * latent
    packed = capacity * HEAD_DIM // 128
    cot = cotangent.reshape(regions, packed, 128)
    vmem = pl.BlockSpec(memory_space=pltpu.VMEM)
    hbm = pl.BlockSpec(memory_space=pl.ANY)
    dma = pltpu.SemaphoreType.DMA
    groups = regions // 8
    pair_grad, projection_grad = pl.pallas_call(
        functools.partial(kernel, regions, columns),
        name="region_backward",
        out_shape=(
            jax.ShapeDtypeStruct((2, HEAD_DIM, latent), F32),
            jax.ShapeDtypeStruct((HEAD_DIM, width), F32),
        ),
        in_specs=[pl.BlockSpec(memory_space=pltpu.SMEM), hbm, hbm, vmem, vmem],
        out_specs=(vmem, vmem),
        scratch_shapes=[
            pltpu.VMEM((regions, capacity, width), BF16),
            pltpu.VMEM((regions, packed, 128), BF16),
            pltpu.VMEM((2, HEAD_DIM, latent), BF16),
            pltpu.VMEM((reach, 2 * HEAD_DIM), BF16),
            pltpu.VMEM((2 * HEAD_DIM, reach), BF16),
            pltpu.VMEM((2 * HEAD_DIM, width), BF16),
            pltpu.VMEM((reach, 2 * HEAD_DIM), F32),
            pltpu.VMEM((HEAD_DIM, width), F32),
            [pltpu.VMEM((reach, 8 * capacity), F32)] * 2,
            [pltpu.VMEM((reach, 8 * capacity), BF16)] * 2,
            [pltpu.VMEM((8 * capacity, 2 * HEAD_DIM), BF16)] * 2,
            [pltpu.VMEM((8, 4 * capacity), F32)] * 2,
            pltpu.VMEM((2, HEAD_DIM, latent), BF16),
            pltpu.VMEM((2, HEAD_DIM, latent), BF16),
            pltpu.VMEM((8, 8, 128), F32),
            pltpu.VMEM((7, 8, 128), F32),
            pltpu.VMEM((groups, 8, 128), F32),
            pltpu.VMEM((8, 8, 128), F32),
            dma((regions,)),
            dma((regions,)),
            dma((regions // columns,)),
            dma((regions,)),
            dma,
            dma((1,)),
            dma((2,)),
            dma((2,)),
            dma((2, 7)),
            dma((2, groups)),
            dma((2, 8)),
        ],
        compiler_params=pltpu.CompilerParams(collective_id=0, has_side_effects=True),
    )(counts, observations[0], cot, keys_values, query_weight)
    return (pair_grad, projection_grad)


def solution(mesh):
    in_specs = (
        P("region", None, None, None),
        P("region", None, "mp", None),
        P(None, "mp", "region"),
        P("mp", None),
        P(),
    )
    out_specs = (P(None, "mp", "region"), P("mp", None))
    return jax.shard_map(
        per_device, mesh=mesh, in_specs=in_specs, out_specs=out_specs, check_vma=False
    )
```

time: 125 us -> 112 us (0.90)
  Pallas kernels: 119 us -> 106 us
    pallas_call x1, Pallas kernels: 119 us -> 106 us  [per_device(): pl.pallas_call(functools.partial(kernel, regions, columns), name='region_...]
where the time goes in v2:
time: 112 us; the launch traced here: 111 us
  Pallas kernels  106 us (95%)
  local copies, waits for them, and re-layouts  4.63 us (4%)
    pallas_call x1, Pallas kernels, per_device(): pl.pallas_call(functools.partial(kernel, regions, columns), name='region_...  106 us
    unnamed x3, local copies, waits for them, and re-layouts  4.63 us

profile of v2, /device:TPU:1, one launch (start us, length us, event | category | flops | bytes accessed | tf_op | source)
XLA Modules:
  0.0 111.5 jit_solution(3463849557566562529)
XLA Ops:
  0.6 1.7 %copy.7 = bf16[8,8,16,128]{3,2,1,0:T(8,128)(2,1)} copy(bf16[8,8,16,128]{3,1,2,0:T(8,128)(2,1)} %bitcast.8) | data formatting | bytes 524288
  2.3 106.2 %region_backward.1 = (f32[2,32,512]{2,1,0:T(8,128)}, f32[32,256]{1,0:T(8,128)}) custom-call(s32[64,64]{1,0:T(8,128)} %counts_ref.1, bf16[64,64,256]{2,1,0:T(8,128)(2,1)} %bitcast.6, bf16[64,16,128]{2,1,0:T(8,128)(2,1)} %bitcast.7, bf16[2,32,512]{2,1,0:T(8,128)(2,1)} %kv_ref.1, bf16[32,256]{1,0:T(8,128)(2,1)} %weight_ref.1), custom_call_target="tpu_custom_call" | custom-call | tf_op jit(solution)/shard_map/region_backward/pallas_call | solution.py:482
  108.5 1.6 %copy.10 = f32[2,32,512]{2,1,0:T(8,128)} copy(f32[2,32,512]{2,1,0:T(8,128)} %get-tuple-element.4) | data formatting | bytes 262144
  110.1 1.4 %copy.11 = f32[32,256]{1,0:T(8,128)} copy(f32[32,256]{1,0:T(8,128)} %get-tuple-element.5) | data formatting | bytes 65536

commit v3 on v2

--- a/solution.py
+++ b/solution.py
@@ -97,14 +97,6 @@
     own_obs.start()
     own_cot.start()
 
-    reach_cols[:HEAD_DIM, :latent] = kv_ref[0]
-    reach_cols[HEAD_DIM:, :latent] = kv_ref[1]
-    weight_rows[:HEAD_DIM] = weight_ref[...]
-    weight_rows[HEAD_DIM:] = jnp.zeros_like(weight_ref)
-    reach_acc[...] = jnp.zeros_like(reach_acc)
-    proj_acc[...] = jnp.zeros_like(proj_acc)
-    for ref in (*scores_buf, *grads_buf, *rows_buf, *top_buf):
-        ref[...] = jnp.zeros_like(ref)
     pl.semaphore_wait(barrier, regions - 1 + 2 * (across - 1))
     kv_copy = pltpu.make_async_remote_copy(
         src_ref=kv_ref,
@@ -139,8 +131,8 @@
         )
 
     kv_copy.start()
-    for t in range(regions // columns):
-        peer = (col - me + regions * columns) % columns + columns * t
+    def send_obs(share):
+        peer = (me + (col - 2 * me + 2 * regions) % columns + columns * share) % regions
 
         @pl.when(peer != me)
         def _():
@@ -152,6 +144,10 @@
             cot_copy(my_chip + chips - k, core).start()
         return carry
 
+    send_obs(0)
+    send_obs(3)
+    send_obs(1)
+    send_obs(2)
     cot_copy(my_chip, 1 - my_core).start()
     lax.fori_loop(1, chips // 2, send_at_distance, 0)
     for core in range(2):
@@ -163,6 +159,14 @@
     def wait_cot(slot):
         pltpu.make_async_copy(cot_hbm.at[0], cot_buf.at[slot], cot_recv.at[slot]).wait()
 
+    reach_cols[:HEAD_DIM, :latent] = kv_ref[0]
+    reach_cols[HEAD_DIM:, :latent] = kv_ref[1]
+    weight_rows[:HEAD_DIM] = weight_ref[...]
+    weight_rows[HEAD_DIM:] = jnp.zeros_like(weight_ref)
+    reach_acc[...] = jnp.zeros_like(reach_acc)
+    proj_acc[...] = jnp.zeros_like(proj_acc)
+    for ref in (*scores_buf, *grads_buf, *rows_buf, *top_buf):
+        ref[...] = jnp.zeros_like(ref)
     kv_copy.wait_recv()
     reach_cols[:HEAD_DIM, latent:] = kv_next[0]
     reach_cols[HEAD_DIM:, latent:] = kv_next[1]
@@ -248,7 +252,7 @@
     def fold_rows(value):
         return value.reshape(chunk // 8, 8, rows)
 
-    def compute(block, last, even):
+    def compute(block, last, even, front=True, middle=True):
         scores_now, scores_before = scores_buf[even], scores_buf[1 - even]
         grads_now, grads_before = grads_buf[1 - even], grads_buf[even]
         rows_ref = rows_buf[even]
@@ -258,10 +262,11 @@
         query_grad = jnp.zeros((HEAD_DIM, rows), F32)
         for index in range(chunks):
             where = slice(index * chunk, (index + 1) * chunk)
-            powers = jnp.exp2((scores_before[where, :rows] - top) * power_scale)
-            scores_before[where, :rows] = powers
-            total = total + jnp.sum(fold_rows(powers), axis=0)
-            row_dot = row_dot + jnp.sum(fold_rows(powers * scores_before[where, rows:]), axis=0)
+            if middle:
+                powers = jnp.exp2((scores_before[where, :rows] - top) * power_scale)
+                scores_before[where, :rows] = powers
+                total = total + jnp.sum(fold_rows(powers), axis=0)
+                row_dot = row_dot + jnp.sum(fold_rows(powers * scores_before[where, rows:]), axis=0)
             reach_acc[where] += jnp.dot(
                 grads_before[where], rows_ref[...], preferred_element_type=F32
             )
@@ -272,7 +277,7 @@
                     grads_before[pair, :rows],
                     preferred_element_type=F32,
                 )
-            if index == 1:
+            if front and index == 1:
                 cot = cot_buf[pl.ds(block * 4, 4)].reshape(4 * packed, cot_buf.shape[2])
                 query = lax.dot_general(
                     block_obs(block),
@@ -287,30 +292,35 @@
                     keep = jnp.logical_and(band, row < live)
                     pieces.append(jnp.where(keep, wide[part * slots : (part + 1) * slots], 0.0))
                 wide = jnp.concatenate(pieces, axis=0).astype(BF16)
-            if index == 4:
+            if front and index == 4:
                 grads = jnp.dot(wide, fold, preferred_element_type=F32).astype(BF16)
-        rows_ref[:rows] = query
-        rows_ref[rows:] = grads
-        both = jnp.concatenate([query, grads], axis=0)
-        inverse = 1.0 / jnp.sum(total, axis=0, keepdims=True)
-        row_dot = jnp.sum(row_dot, axis=0, keepdims=True) * inverse
+        if front:
+            rows_ref[:rows] = query
+            rows_ref[rows:] = grads
+            both = jnp.concatenate([query, grads], axis=0)
+        if middle:
+            inverse = 1.0 / jnp.sum(total, axis=0, keepdims=True)
+            row_dot = jnp.sum(row_dot, axis=0, keepdims=True) * inverse
         query_grad = (query_grad * scale_back).astype(BF16)
         highest = None
         for index in range(chunks):
             where = slice(index * chunk, (index + 1) * chunk)
-            products = lax.dot_general(
-                reach_rows[where], both, (((1,), (1,)), ((), ())), preferred_element_type=F32
-            )
-            scores_now[where] = products
-            here = jnp.max(fold_rows(products[:, :rows]), axis=0)
-            highest = here if highest is None else jnp.maximum(highest, here)
-            attention = scores_before[where, :rows] * inverse
-            score_grad = attention * (scores_before[where, rows:] - row_dot)
-            grads_now[where, :rows] = score_grad.astype(BF16)
-            grads_now[where, rows:] = attention.astype(BF16)
+            if front:
+                products = lax.dot_general(
+                    reach_rows[where], both, (((1,), (1,)), ((), ())), preferred_element_type=F32
+                )
+                scores_now[where] = products
+                here = jnp.max(fold_rows(products[:, :rows]), axis=0)
+                highest = here if highest is None else jnp.maximum(highest, here)
+            if middle:
+                attention = scores_before[where, :rows] * inverse
+                score_grad = attention * (scores_before[where, rows:] - row_dot)
+                grads_now[where, :rows] = score_grad.astype(BF16)
+                grads_now[where, rows:] = attention.astype(BF16)
             if index == 3:
                 proj_acc[...] += jnp.dot(query_grad, block_obs(last), preferred_element_type=F32)
-        top_buf[even][...] = highest
+        if front:
+            top_buf[even][...] = highest
 
     def at(index):
         return (jnp.clip(index, 0, blocks - 1) + 1) % blocks
@@ -339,7 +349,9 @@
             stage(pair * 2 + even, even)
         return carry
 
-    lax.fori_loop(0, (blocks + 2 + SECOND_LAG) // 2, stages, 0)
+    lax.fori_loop(0, (blocks + SECOND_LAG) // 2, stages, 0)
+    compute(0, at(blocks - 2), 0, front=False)
+    compute(0, at(blocks - 1), 1, front=False, middle=False)
 
     group = me // 8
     member = me % 8
@@ -464,6 +476,11 @@
         final_copy(i).wait_send()
     for i in range(1, groups):
         group_copy(i).wait_send()
+
+
+def hand_over(pair_in, proj_in, pair_out, proj_out):
+    pair_out[...] = pair_in[...]
+    proj_out[...] = proj_in[...]
 
 
 def per_device(observations, cotangent, keys_values, query_weight, counts):
@@ -521,7 +538,16 @@
         ],
         compiler_params=pltpu.CompilerParams(collective_id=0, has_side_effects=True),
     )(counts, observations[0], cot, keys_values, query_weight)
-    return (pair_grad, projection_grad)
+    return pl.pallas_call(
+        hand_over,
+        name="hand_over",
+        out_shape=(
+            jax.ShapeDtypeStruct(pair_grad.shape, F32),
+            jax.ShapeDtypeStruct(projection_grad.shape, F32),
+        ),
+        in_specs=[vmem, vmem],
+        out_specs=(vmem, vmem),
+    )(pair_grad, projection_grad)
 
 
 def solution(mesh):

time: 112 us -> 106 us (0.946)
  local copies, waits for them, and re-layouts: 4.63 us -> 1.69 us
  Pallas kernels: 106 us -> 104 us
    pallas_call x1, Pallas kernels: 106 us -> 102 us  [per_device(): pl.pallas_call(functools.partial(kernel, regions, columns), name='region_...]
    unnamed x3 -> x1, local copies, waits for them, and re-layouts: 4.63 us -> 1.69 us
    pallas_call x0 -> x1, Pallas kernels: none -> 1.57 us  [per_device(): pl.pallas_call(hand_over, name='hand_over', out_shape=(jax.ShapeDtypeStru...]
where the time goes in v3:
time: 106 us
  Pallas kernels  104 us (98%)
  local copies, waits for them, and re-layouts  1.69 us (2%)
    pallas_call x1, Pallas kernels, per_device(): pl.pallas_call(functools.partial(kernel, regions, columns), name='region_...  102 us

profile of v3, /device:TPU:1, one launch (start us, length us, event | category | flops | bytes accessed | tf_op | source)
XLA Modules:
  0.0 105.9 jit_solution(6218186937774669907)
XLA Ops:
  0.6 1.7 %copy.7 = bf16[8,8,16,128]{3,2,1,0:T(8,128)(2,1)} copy(bf16[8,8,16,128]{3,1,2,0:T(8,128)(2,1)} %bitcast.8) | data formatting | bytes 524288
  2.3 102.0 %region_backward.1 = (f32[2,32,512]{2,1,0:T(8,128)}, f32[32,256]{1,0:T(8,128)}) custom-call(s32[64,64]{1,0:T(8,128)} %counts_ref.1, bf16[64,64,256]{2,1,0:T(8,128)(2,1)} %bitcast.6, bf16[64,16,128]{2,1,0:T(8,128)(2,1)} %bitcast.7, bf16[2,32,512]{2,1,0:T(8,128)(2,1)} %kv_ref.1, bf16[32,256]{1,0:T(8,128)(2,1)} %weight_ref.1), custom_call_target="tpu_custom_call" | custom-call | tf_op jit(solution)/shard_map/region_backward/pallas_call | solution.py:499
  104.3 1.6 %hand_over.1 = (f32[2,32,512]{2,1,0:T(8,128)}, f32[32,256]{1,0:T(8,128)}) custom-call(f32[2,32,512]{2,1,0:T(8,128)} %get-tuple-element.4.pair_in, f32[32,256]{1,0:T(8,128)} %get-tuple-element.5.proj_in), custom_call_target="tpu_custom_call" | custom-call | tf_op jit(solution)/shard_map/hand_over/pallas_call | solution.py:541

commit v4 on v3

--- a/solution.py
+++ b/solution.py
@@ -26,13 +26,16 @@
 def kernel(
     regions,
     columns,
-    counts_ref,
+    counts_hbm,
     obs_hbm,
     cot_hbm,
+    kv_hbm,
+    weight_hbm,
+    pair_ref,
+    proj_ref,
+    counts_ref,
     kv_ref,
     weight_ref,
-    pair_ref,
-    proj_ref,
     obs_buf,
     cot_buf,
     kv_next,
@@ -56,7 +59,7 @@
     obs_send,
     relay_send,
     cot_send,
-    own_sem,
+    own_sems,
     kv_sems,
     edge_sems,
     part_sems,
@@ -68,7 +71,7 @@
     col = lax.axis_index("mp")
     my_chip = me // 2
     my_core = me % 2
-    latent = kv_ref.shape[2]
+    latent = kv_hbm.shape[2]
     blocks = regions // 4
 
     across = 4
@@ -84,22 +87,30 @@
         pl.semaphore_signal(sem, inc=1, device_id=(region, column), device_id_type=MESH)
 
     def greet_region(i, carry):
-        tell(barrier, (me + i) % regions, col)
+        offset = regions // 2 + (1 - 2 * (i % 2)) * ((i + 1) // 2)
+        tell(barrier, (me + offset) % regions, col)
         return carry
 
-    lax.fori_loop(1, regions, greet_region, 0)
+    lax.fori_loop(0, regions - 1, greet_region, 0)
     for i in range(1, across):
         tell(barrier, me, along_x(i))
         tell(barrier, me, along_y(i))
     own_slot = my_core
     own_obs = pltpu.make_async_copy(obs_hbm.at[me], obs_buf.at[own_slot], obs_recv.at[own_slot])
     own_cot = pltpu.make_async_copy(cot_hbm.at[me], cot_buf.at[own_slot], cot_recv.at[own_slot])
+    local = [
+        pltpu.make_async_copy(counts_hbm, counts_ref, own_sems.at[0]),
+        pltpu.make_async_copy(kv_hbm, kv_ref, own_sems.at[1]),
+        pltpu.make_async_copy(weight_hbm, weight_ref, own_sems.at[2]),
+    ]
+    for copy in local:
+        copy.start()
     own_obs.start()
     own_cot.start()
 
     pl.semaphore_wait(barrier, regions - 1 + 2 * (across - 1))
     kv_copy = pltpu.make_async_remote_copy(
-        src_ref=kv_ref,
+        src_ref=kv_hbm,
         dst_ref=kv_next,
         send_sem=kv_sems.at[0],
         recv_sem=kv_sems.at[1],
@@ -118,9 +129,8 @@
             device_id_type=MESH,
         )
 
-    def cot_copy(chip, core):
+    def cot_copy(chip, core, slot):
         peer = (chip % chips) * 2 + core
-        slot = slot_of(me, peer, chips)
         return pltpu.make_async_remote_copy(
             src_ref=cot_hbm.at[peer],
             dst_ref=cot_buf.at[slot],
@@ -140,18 +150,18 @@
 
     def send_at_distance(k, carry):
         for core in range(2):
-            cot_copy(my_chip + k, core).start()
-            cot_copy(my_chip + chips - k, core).start()
+            cot_copy(my_chip + k, core, k * 4 + 2 + my_core).start()
+            cot_copy(my_chip + chips - k, core, k * 4 + my_core).start()
         return carry
 
     send_obs(0)
     send_obs(3)
     send_obs(1)
     send_obs(2)
-    cot_copy(my_chip, 1 - my_core).start()
+    cot_copy(my_chip, 1 - my_core, my_core).start()
     lax.fori_loop(1, chips // 2, send_at_distance, 0)
     for core in range(2):
-        cot_copy(my_chip + chips // 2, core).start()
+        cot_copy(my_chip + chips // 2, core, 2 + my_core).start()
 
     def wait_obs(slot):
         pltpu.make_async_copy(obs_hbm.at[0], obs_buf.at[slot], obs_recv.at[slot]).wait()
@@ -159,6 +169,8 @@
     def wait_cot(slot):
         pltpu.make_async_copy(cot_hbm.at[0], cot_buf.at[slot], cot_recv.at[slot]).wait()
 
+    for copy in local:
+        copy.wait()
     reach_cols[:HEAD_DIM, :latent] = kv_ref[0]
     reach_cols[HEAD_DIM:, :latent] = kv_ref[1]
     weight_rows[:HEAD_DIM] = weight_ref[...]
@@ -409,7 +421,7 @@
             device_id_type=MESH,
         )
 
-    for i in range(1, groups):
+    for i in sorted(range(1, groups), key=lambda i: -min(i, groups - i)):
         group_copy(i).start()
 
     def sent_block(block, carry):
@@ -503,9 +515,12 @@
             jax.ShapeDtypeStruct((2, HEAD_DIM, latent), F32),
             jax.ShapeDtypeStruct((HEAD_DIM, width), F32),
         ),
-        in_specs=[pl.BlockSpec(memory_space=pltpu.SMEM), hbm, hbm, vmem, vmem],
+        in_specs=[hbm] * 5,
         out_specs=(vmem, vmem),
         scratch_shapes=[
+            pltpu.SMEM(counts.shape, jnp.int32),
+            pltpu.VMEM((2, HEAD_DIM, latent), BF16),
+            pltpu.VMEM((HEAD_DIM, width), BF16),
             pltpu.VMEM((regions, capacity, width), BF16),
             pltpu.VMEM((regions, packed, 128), BF16),
             pltpu.VMEM((2, HEAD_DIM, latent), BF16),
@@ -529,7 +544,7 @@
             dma((regions // columns,)),
             dma((regions,)),
             dma,
-            dma((1,)),
+            dma((3,)),
             dma((2,)),
             dma((2,)),
             dma((2, 7)),

time: 106 us -> 104 us (0.981)
  Pallas kernels: 104 us -> 102 us
    pallas_call x1, Pallas kernels: 102 us -> 100 us  [per_device(): pl.pallas_call(functools.partial(kernel, regions, columns), name='region_...]
where the time goes in v4:
time: 104 us
  Pallas kernels  102 us (98%)
  local copies, waits for them, and re-layouts  1.69 us (2%)
    pallas_call x1, Pallas kernels, per_device(): pl.pallas_call(functools.partial(kernel, regions, columns), name='region_...  100 us

profile of v4, /device:TPU:1, one launch (start us, length us, event | category | flops | bytes accessed | tf_op | source)
XLA Modules:
  0.0 103.9 jit_solution(238847150042463425)
XLA Ops:
  0.6 1.7 %copy.7 = bf16[8,8,16,128]{3,2,1,0:T(8,128)(2,1)} copy(bf16[8,8,16,128]{3,1,2,0:T(8,128)(2,1)} %bitcast.8) | data formatting | bytes 524288
  2.3 100.0 %region_backward.1 = (f32[2,32,512]{2,1,0:T(8,128)}, f32[32,256]{1,0:T(8,128)}) custom-call(s32[64,64]{1,0:T(8,128)} %counts_hbm.1, bf16[64,64,256]{2,1,0:T(8,128)(2,1)} %bitcast.6, bf16[64,16,128]{2,1,0:T(8,128)(2,1)} %bitcast.7, bf16[2,32,512]{2,1,0:T(8,128)(2,1)} %kv_hbm.1, bf16[32,256]{1,0:T(8,128)(2,1)} %weight_hbm.1), custom_call_target="tpu_custom_call" | custom-call | tf_op jit(solution)/shard_map/region_backward/pallas_call | solution.py:511
  102.4 1.6 %hand_over.1 = (f32[2,32,512]{2,1,0:T(8,128)}, f32[32,256]{1,0:T(8,128)}) custom-call(f32[2,32,512]{2,1,0:T(8,128)} %get-tuple-element.4.pair_in, f32[32,256]{1,0:T(8,128)} %get-tuple-element.5.proj_in), custom_call_target="tpu_custom_call" | custom-call | tf_op jit(solution)/shard_map/hand_over/pallas_call | solution.py:556
